TPU v7x, 256 devices: a whole 4x4x8 slice. The times are simulated.
256 devices in a mesh: wide: 32 (over y_lo, z, core), narrow: 8 (over x, y_hi).
Axes of the slice: x: 4, y: 4 (y_hi: 2, y_lo: 2; y = y_hi * 2 + y_lo), z: 8, core: 2. Of those that a mesh axis runs over, the one named last changes fastest.
Arguments:
- dark: bfloat16 [64, 32, 8, 16], P(None, None, 'narrow'), may hold values from -6 to 6
- w_enc: bfloat16 [27, 64, 64], replicated, may hold values from -0.15625 to 0.15625
- up_weight: bfloat16 [512, 16, 64], replicated, may hold values from -0.75 to 0.75
- w_dec: bfloat16 [27, 16, 16], replicated, may hold values from -0.3125 to 0.3125
- cotangent: bfloat16 [16, 256, 64, 128], P(None, 'wide', 'narrow'), may hold values from -6 to 6
Outputs:
- grad_dark: float32 [64, 32, 8, 16], P(None, None, 'narrow')
- grad_w_enc: float32 [27, 64, 64], replicated
- grad_up_weight: float32 [512, 16, 64], P(('wide', 'narrow'))
- grad_w_dec: float32 [27, 16, 16], replicated
All inputs are finite; a program needn't handle non-finite values.
Results may differ from a plain program's by a relative error of at most 0.0053.
Values may be sent and summed in bfloat16 or wider, within the bound.
A program may use at most 64 MiB of HBM per device.

v0:
```python
import math

import jax
import jax.numpy as jnp
from jax import lax
from jax.sharding import PartitionSpec as P

RATIO = 8


def padded_2(block, sides, width):
    for axis, dim in sides:
        count = lax.axis_size(axis)
        forward = [(i, i + 1) for i in range(count - 1)]
        backward = [(target, source) for source, target in forward]
        low = lax.ppermute(
            lax.slice_in_dim(block, block.shape[dim] - width, None, axis=dim), axis, forward
        )
        high = lax.ppermute(lax.slice_in_dim(block, 0, width, axis=dim), axis, backward)
        block = jnp.concatenate([low, block, high], axis=dim)
    return block


def silu_slope(values):
    sigma = jax.nn.sigmoid(values)
    return sigma * (1.0 + values * (1.0 - sigma))


def coarse_margin(field):
    return padded_2(field, (("narrow", 2),), 1)


def pad_coarse(field):
    return jnp.pad(field, ((0, 0), (1, 1), (0, 0), (1, 1)))


def pad_fine(field):
    return jnp.pad(field, ((0, 0), (0, 0), (0, 0), (1, 1)))


def flatten(kernel):
    return kernel.transpose(1, 0, 2).reshape(kernel.shape[1], -1)


def transposed(kernel):
    return kernel[::-1].transpose(2, 0, 1).reshape(kernel.shape[2], -1)


def unflatten(flat):
    return flat.reshape(flat.shape[0], 27, -1).transpose(1, 0, 2)


def columns(padded, first, count, depth, width):
    pieces = []
    for shift_x in range(3):
        for shift_z in range(3):
            for shift_y in range(3):
                pieces.append(
                    padded[
                        :,
                        first + shift_x : first + shift_x + count,
                        shift_z : shift_z + depth,
                        shift_y : shift_y + width,
                    ]
                )
    return jnp.concatenate(pieces, 0)


def block_size(planes):
    return planes // 4


def convolve_blocks(padded, flat):
    planes = padded.shape[1] - 2
    depth = padded.shape[2] - 2
    width = padded.shape[3] - 2
    block = block_size(planes)
    results = []
    for first in range(0, planes, block):
        stacked = columns(padded, first, block, depth, width)
        results.append(
            jnp.einsum("ok,kxzy->oxzy", flat, stacked, preferred_element_type=jnp.float32)
        )
    return jnp.concatenate(results, 1)


def upsample(table, enc_planes, ratio, fine_ch):
    chans = enc_planes.shape[0]
    planes = enc_planes.shape[1]
    depth = enc_planes.shape[2]
    width = enc_planes.shape[3]
    up_rows = jnp.dot(
        table, enc_planes.reshape(chans, planes * depth * width), preferred_element_type=jnp.float32
    )
    return (
        up_rows.reshape(ratio, ratio, ratio, fine_ch, planes, depth, width)
        .transpose(3, 4, 0, 5, 1, 6, 2)
        .reshape(fine_ch, planes * ratio, depth * ratio, width * ratio)
        .astype(jnp.bfloat16)
    )


def on_device(dark, w_enc, up_weight, w_dec, cotangent):
    ratio = RATIO
    chans = dark.shape[0]
    fine_ch = w_dec.shape[1]
    subs = up_weight.shape[0]
    wide_count = lax.axis_size("wide")
    narrow_count = lax.axis_size("narrow")
    coarse_planes = dark.shape[1]
    own_planes = coarse_planes // wide_count
    depth = dark.shape[2]
    width = dark.shape[3]
    first_plane = lax.axis_index("wide") * own_planes
    dark_padded = pad_coarse(coarse_margin(dark))
    enc_flat_kernel = flatten(w_enc)
    enc_pre = convolve_blocks(dark_padded, enc_flat_kernel)
    encoded = jax.nn.silu(enc_pre).astype(jnp.bfloat16)
    enc_window = lax.dynamic_slice_in_dim(
        jnp.pad(encoded, ((0, 0), (1, 1), (0, 0), (0, 0))), first_plane, own_planes + 2, 1
    )
    enc_own = enc_window[:, 1 : own_planes + 1]
    cells = own_planes * depth * width
    enc_flat = enc_own.reshape(chans, cells)
    table = up_weight.reshape(subs * fine_ch, chans)
    fine_planes = own_planes * ratio
    fine_depth = depth * ratio
    fine_width = width * ratio
    upsampled = upsample(table, enc_own, ratio, fine_ch)
    up_padded = pad_fine(padded_2(upsampled, (("wide", 1), ("narrow", 2)), 1))
    dec_flat = flatten(w_dec)
    cot_float = cotangent.astype(jnp.float32)
    block = block_size(fine_planes)
    grad_pieces = []
    dec_total = jnp.zeros((fine_ch, 27 * fine_ch), jnp.float32)
    for first in range(0, fine_planes, block):
        stacked = columns(up_padded, first, block, fine_depth, fine_width)
        pre_block = jnp.einsum(
            "ok,kxzy->oxzy", dec_flat, stacked, preferred_element_type=jnp.float32
        )
        piece = (cot_float[:, first : first + block] * silu_slope(pre_block)).astype(jnp.bfloat16)
        dec_total = dec_total + jnp.einsum(
            "oxzy,kxzy->ok", piece, stacked, preferred_element_type=jnp.float32
        )
        grad_pieces.append(piece)
    dec_grad = jnp.concatenate(grad_pieces, 1)
    grad_padded = pad_fine(padded_2(dec_grad, (("wide", 1), ("narrow", 2)), 1))
    back_up = convolve_blocks(grad_padded, transposed(w_dec))
    up_grad = (cot_float + back_up).astype(jnp.bfloat16)
    grad_rows = (
        up_grad.reshape(fine_ch, own_planes, ratio, depth, ratio, width, ratio)
        .transpose(2, 4, 6, 0, 1, 3, 5)
        .reshape(subs * fine_ch, cells)
    )
    enc_grad_own = (
        jnp.einsum("kc,kn->cn", table, grad_rows, preferred_element_type=jnp.float32)
        .reshape(chans, own_planes, depth, width)
        .astype(jnp.bfloat16)
    )
    enc_grad = lax.all_gather(enc_grad_own, "wide", axis=1, tiled=True)
    enc_pre_grad = (enc_grad.astype(jnp.float32) * silu_slope(enc_pre)).astype(jnp.bfloat16)
    grad_own = lax.dynamic_slice_in_dim(enc_pre_grad, first_plane, own_planes, 1)
    dark_own = lax.dynamic_slice_in_dim(dark_padded, first_plane, own_planes + 2, 1)
    stacked_own = columns(dark_own, 0, own_planes, depth, width)
    enc_total = jnp.einsum(
        "oxzy,kxzy->ok", grad_own, stacked_own, preferred_element_type=jnp.float32
    )
    grad_dark = convolve_blocks(pad_coarse(coarse_margin(enc_pre_grad)), transposed(w_enc))
    coarse_count = coarse_planes * depth * narrow_count * width
    coarse_scale = 1.0 / math.sqrt(coarse_count)
    fine_scale = 1.0 / math.sqrt(coarse_count * subs)
    owners = wide_count * narrow_count
    own_rows = subs // owners
    enc_sum, dec_sum, up_sum = lax.psum(
        (
            enc_total,
            dec_total,
            jnp.einsum(
                "kn,cn->kc", grad_rows, enc_flat, preferred_element_type=jnp.float32
            ).reshape(subs, fine_ch, chans),
        ),
        ("wide", "narrow"),
    )
    up_own = lax.dynamic_slice_in_dim(
        up_sum, lax.axis_index(("wide", "narrow")) * own_rows, own_rows, 0
    )
    return (
        grad_dark,
        unflatten(enc_sum) * coarse_scale,
        up_own * coarse_scale,
        unflatten(dec_sum) * fine_scale,
    )


def solution(mesh):
    in_specs = (P(None, None, "narrow", None), P(), P(), P(), P(None, "wide", "narrow", None))
    out_specs = (P(None, None, "narrow", None), P(), P(("wide", "narrow"), None, None), P())
    return jax.shard_map(
        on_device, mesh=mesh, in_specs=in_specs, out_specs=out_specs, check_vma=False
    )
```

profile of v0, /device:TPU:1, one launch (start us, length us, event | category | flops | bytes accessed | tf_op | source)
XLA Modules:
  0.0 538.3 jit_solution(12176044866597356027)
XLA Ops:
  7.2 5.6 %collective-permute-start = (bf16[64,32,1,16]{0,3,1,2:T(8,128)(2,1)}, bf16[64,32,1,16]{0,3,1,2:T(8,128)(2,1)S(1)}, u32[]{:S(2)}, u32[]{:S(2)}) collective-permute-start(bf16[64,32,1,16]{0,3,1,2:T(8,128)(2,1)} %bitcast.228), channel_id=1, source_target_pairs={{0,1},{1,2},{2,3},{3,4},{4,5},{5,6},{6,7},{8,9},{9,10},{10,11},{11... | collective-permute-start | bytes 196616 | tf_op jit(solution)/shard_map/ppermute | solution.py:16
  12.9 1.3 collective-permute-start.1
  14.2 1.6 fusion.88
  15.8 1.3 copy.39
  17.5 3.0 copy.48
  26.4 1.7 fusion.87
  28.8 2.0 concatenate.180
  30.8 1.3 convolution_bitcast_fusion.15
  32.1 2.0 concatenate.182
  34.2 1.3 convolution_bitcast_fusion.14
  35.5 2.0 concatenate.184
  37.6 1.3 convolution_bitcast_fusion.13
  38.9 2.0 concatenate.186
  40.8 1.3 convolution_bitcast_fusion.12
  43.4 2.7 convert_element_type.71
  46.1 3.5 copy.96
  49.6 1.9 copy.50
  52.2 4.7 collective-permute-start.2
  56.9 1.9 collective-permute-start.3
  60.8 1.5 rev.6
  62.3 1.7 copy.56
  64.0 1.7 reshape.355
  65.7 1.7 copy.63
  68.5 1.3 pad_maximum_fusion.13
  69.8 6.0 %collective-permute-start.4 = (bf16[16,10,1,128]{3,0,2,1:T(8,128)(2,1)}, bf16[16,10,1,128]{3,0,2,1:T(8,128)(2,1)}, u32[]{:S(2)}, u32[]{:S(2)}) collective-permute-start(bf16[16,10,1,128]{3,0,2,1:T(8,128)(2,1)} %get-tuple-element.286), channel_id=1, source_target_pairs={{0,1},{1,2},{2,3},{3,4},{4,5},{5,6},{6,7},{8,9},{9,10},{10,11},{11... | collective-permute-start | bytes 122888 | tf_op jit(solution)/shard_map/ppermute | solution.py:16
  75.8 1.3 collective-permute-start.5
  77.9 1.5 concatenate.219
  79.4 3.0 collective-permute-done.5
  82.4 1.3 fusion.17
  88.4 5.3 collective-permute-start.6
  98.7 1.9 collective-permute-start.7
  100.7 80.2 %psum.23 = f32[16,432]{1,0:T(8,128)S(1)} all-reduce(f32[16,432]{1,0:T(8,128)S(1)} %fusion.7), channel_id=1, replica_groups=mesh['wide'=32,'narrow'=8] {'wide','narrow'}, use_global_device_ids=true, to_apply=%region_2.3 | all-reduce | flops 6912 | bytes 55296 | tf_op jit(solution)/shard_map/psum | solution.py:174
  181.5 3.1 collective-permute-start.8
  184.6 1.3 collective-permute-start.9
  188.3 2.8 collective-permute-done.9
  198.5 1.8 copy.64
  200.2 4.1 copy.70
  204.4 3.5 copy.65
  207.9 4.7 reshape.344
  213.0 36.5 %all-gather = bf16[64,512]{0,1:T(8,128)(2,1)S(1)} all-gather(bf16[64,16]{0,1:T(8,128)(2,1)S(1)} %fusion.10), channel_id=2, replica_groups=mesh['wide'=32,'narrow'=8] {'wide'}, dimensions={1}, use_global_device_ids=true | all-gather | bytes 67584 | tf_op jit(solution)/shard_map/all_gather | solution.py:160
  249.7 3.6 collective-permute-start.10
  253.3 1.5 collective-permute-start.11
  254.9 2.8 fusion.1
  258.8 2.5 collective-permute-done.11
  264.7 1.3 concatenate.214
  265.9 1.3 concatenate.215
  271.3 255.8 %all-reduce.8.cloned.1.call-done = (f32[64,1728]{1,0:T(8,128)}, f32[512,16,64]{2,0,1:T(8,128)}) async-done(((f32[64,1728]{1,0:T(8,128)}, f32[512,16,64]{2,0,1:T(8,128)}), (f32[64,1728]{1,0:T(8,128)}, f32[512,16,64]{2,0,1:T(8,128)})) %all-reduce.8.cloned.1.call-update) | async-done | bytes 2539536 | tf_op jit(solution)/shard_map/psum | solution.py:174
  528.6 1.4 copy.73
  (280 shorter events, 43.9 us)
Async XLA Ops:
  7.2 519.9 %all-reduce.8.cloned.1.call-start = ((), (), s32[]{:S(2)}) async-start(), calls=%async_computation | async-start | bytes 9306112 | tf_op jit(solution)/shard_map/psum | solution.py:174
  7.2 13.3 %collective-permute-start = (bf16[64,32,1,16]{0,3,1,2:T(8,128)(2,1)}, bf16[64,32,1,16]{0,3,1,2:T(8,128)(2,1)S(1)}, u32[]{:S(2)}, u32[]{:S(2)}) collective-permute-start(bf16[64,32,1,16]{0,3,1,2:T(8,128)(2,1)} %bitcast.228), channel_id=1, source_target_pairs={{0,1},{1,2},{2,3},{3,4},{4,5},{5,6},{6,7},{8,9},{9,10},{10,11},{11... | collective-permute-start | bytes 196616 | tf_op jit(solution)/shard_map/ppermute | solution.py:16
  12.9 8.4 %collective-permute-start.1 = (bf16[64,32,1,16]{0,3,1,2:T(8,128)(2,1)}, bf16[64,32,1,16]{0,3,1,2:T(8,128)(2,1)}, u32[]{:S(2)}, u32[]{:S(2)}) collective-permute-start(bf16[64,32,1,16]{0,3,1,2:T(8,128)(2,1)} %bitcast.229), channel_id=1, source_target_pairs={{1,0},{2,1},{3,2},{4,3},{5,4},{6,5},{7,6},{9,8},{10,9},{11,10},{12... | collective-permute-start | bytes 196616 | tf_op jit(solution)/shard_map/ppermute | solution.py:19
  17.5 3.7 copy-start.2
  20.6 0.7 copy-start.3
  24.0 4.0 copy-start.4
  26.4 5.8 %copy-start.24 = (bf16[64,8,1,16]{0,3,1,2:T(8,128)(2,1)S(1)}, bf16[64,8,1,16]{0,3,1,2:T(8,128)(2,1)}, u32[]{:S(2)}) copy-start(bf16[64,8,1,16]{0,3,1,2:T(8,128)(2,1)} %get-tuple-element.345) | copy-start | bytes 49156
  26.4 5.8 %copy-start.25 = (bf16[64,8,1,16]{0,3,1,2:T(8,128)(2,1)S(1)}, bf16[64,8,1,16]{0,3,1,2:T(8,128)(2,1)}, u32[]{:S(2)}) copy-start(bf16[64,8,1,16]{0,3,1,2:T(8,128)(2,1)} %get-tuple-element.346) | copy-start | bytes 49156
  26.4 5.8 %copy-start.26 = (bf16[64,8,1,16]{0,3,1,2:T(8,128)(2,1)S(1)}, bf16[64,8,1,16]{0,3,1,2:T(8,128)(2,1)}, u32[]{:S(2)}) copy-start(bf16[64,8,1,16]{0,3,1,2:T(8,128)(2,1)} %get-tuple-element.347) | copy-start | bytes 49156
  30.8 4.7 copy-start.22
  30.8 4.7 copy-start.23
  34.2 4.7 copy-start.21
  35.5 6.7 %copy-start.9 = (f32[64,8,1,16]{0,3,1,2:T(8,128)}, f32[64,8,1,16]{0,3,1,2:T(8,128)S(1)}, u32[]{:S(2)}) copy-start(f32[64,8,1,16]{0,3,1,2:T(8,128)S(1)} %convolution_bitcast_fusion.14) | copy-start | bytes 98308
  38.8 3.4 copy-start.11
  42.1 0.6 copy-start.13
  42.8 3.3 copy-start.5
  49.6 9.2 %copy-start.7 = (bf16[16,8,8,128]{3,2,1,0:T(8,128)(2,1)S(1)}, bf16[16,8,8,128]{3,2,1,0:T(8,128)(2,1)}, u32[]{:S(2)}) copy-start(bf16[16,8,8,128]{3,2,1,0:T(8,128)(2,1)} %param.9) | copy-start | bytes 786436
  52.2 16.3 %collective-permute-start.2 = (bf16[16,1,8,128]{3,0,2,1:T(8,128)(2,1)}, bf16[16,1,8,128]{3,0,2,1:T(8,128)(2,1)}, u32[]{:S(2)}, u32[]{:S(2)}) collective-permute-start(bf16[16,1,8,128]{3,0,2,1:T(8,128)(2,1)} %get-tuple-element.297), channel_id=1, source_target_pairs={{0,8},{8,16},{16,24},{24,32},{32,40},{40,48},{48,56},{56,64},{64,7... | collective-permute-start | bytes 98312 | tf_op jit(solution)/shard_map/ppermute | solution.py:16
  56.9 11.6 %collective-permute-start.3 = (bf16[16,1,8,128]{3,0,2,1:T(8,128)(2,1)}, bf16[16,1,8,128]{3,0,2,1:T(8,128)(2,1)S(1)}, u32[]{:S(2)}, u32[]{:S(2)}) collective-permute-start(bf16[16,1,8,128]{3,0,2,1:T(8,128)(2,1)} %get-tuple-element.298), channel_id=1, source_target_pairs={{8,0},{16,8},{24,16},{32,24},{40,32},{48,40},{56,48},{64,56},{72,6... | collective-permute-start | bytes 98312 | tf_op jit(solution)/shard_map/ppermute | solution.py:19
  69.8 9.6 %collective-permute-start.4 = (bf16[16,10,1,128]{3,0,2,1:T(8,128)(2,1)}, bf16[16,10,1,128]{3,0,2,1:T(8,128)(2,1)}, u32[]{:S(2)}, u32[]{:S(2)}) collective-permute-start(bf16[16,10,1,128]{3,0,2,1:T(8,128)(2,1)} %get-tuple-element.286), channel_id=1, source_target_pairs={{0,1},{1,2},{2,3},{3,4},{4,5},{5,6},{6,7},{8,9},{9,10},{10,11},{11... | collective-permute-start | bytes 122888 | tf_op jit(solution)/shard_map/ppermute | solution.py:16
  75.8 6.6 %collective-permute-start.5 = (bf16[16,10,1,128]{3,0,2,1:T(8,128)(2,1)}, bf16[16,10,1,128]{3,0,2,1:T(8,128)(2,1)}, u32[]{:S(2)}, u32[]{:S(2)}) collective-permute-start(bf16[16,10,1,128]{3,0,2,1:T(8,128)(2,1)} %get-tuple-element.287), channel_id=1, source_target_pairs={{1,0},{2,1},{3,2},{4,3},{5,4},{6,5},{7,6},{9,8},{10,9},{11,10},{12... | collective-permute-start | bytes 122888 | tf_op jit(solution)/shard_map/ppermute | solution.py:19
  86.9 1.0 copy-start.1
  86.9 1.0 copy-start.15
  88.4 6.6 %collective-permute-start.6 = (bf16[16,1,8,128]{3,0,2,1:T(8,128)(2,1)S(1)}, bf16[16,1,8,128]{3,0,2,1:T(8,128)(2,1)S(1)}, u32[]{:S(2)}, u32[]{:S(2)}) collective-permute-start(bf16[16,1,8,128]{3,0,2,1:T(8,128)(2,1)S(1)} %slice.2093), channel_id=1, source_target_pairs={{0,8},{8,16},{16,24},{24,32},{32,40},{40,48},{48,56},{56,64},{64,7... | collective-permute-start | bytes 98312 | tf_op jit(solution)/shard_map/ppermute | solution.py:16
  95.0 0.6 copy-start.19
  98.7 82.2 %collective-permute-start.7 = (bf16[16,1,8,128]{3,0,2,1:T(8,128)(2,1)S(1)}, bf16[16,1,8,128]{3,0,2,1:T(8,128)(2,1)S(1)}, u32[]{:S(2)}, u32[]{:S(2)}) collective-permute-start(bf16[16,1,8,128]{3,0,2,1:T(8,128)(2,1)S(1)} %slice.2150), channel_id=1, source_target_pairs={{8,0},{16,8},{24,16},{32,24},{40,32},{48,40},{56,48},{64,56},{72,6... | collective-permute-start | bytes 98312 | tf_op jit(solution)/shard_map/ppermute | solution.py:19
  180.9 3.7 copy-start.17
  181.5 6.7 %collective-permute-start.8 = (bf16[16,10,1,128]{3,0,2,1:T(8,128)(2,1)}, bf16[16,10,1,128]{3,0,2,1:T(8,128)(2,1)S(1)}, u32[]{:S(2)}, u32[]{:S(2)}) collective-permute-start(bf16[16,10,1,128]{3,0,2,1:T(8,128)(2,1)} %get-tuple-element.282), channel_id=1, source_target_pairs={{0,1},{1,2},{2,3},{3,4},{4,5},{5,6},{6,7},{8,9},{9,10},{10,11},{11... | collective-permute-start | bytes 122888 | tf_op jit(solution)/shard_map/ppermute | solution.py:16
  184.6 6.5 %collective-permute-start.9 = (bf16[16,10,1,128]{3,0,2,1:T(8,128)(2,1)}, bf16[16,10,1,128]{3,0,2,1:T(8,128)(2,1)S(1)}, u32[]{:S(2)}, u32[]{:S(2)}) collective-permute-start(bf16[16,10,1,128]{3,0,2,1:T(8,128)(2,1)} %get-tuple-element.283), channel_id=1, source_target_pairs={{1,0},{2,1},{3,2},{4,3},{5,4},{6,5},{7,6},{9,8},{10,9},{11,10},{12... | collective-permute-start | bytes 122888 | tf_op jit(solution)/shard_map/ppermute | solution.py:19
  188.3 3.4 copy-start.20
  195.5 0.9 copy-start.18
  197.3 1.0 copy-start.8
  212.6 36.9 %copy-start.10 = (f32[64,8,1,16]{0,3,1,2:T(8,128)S(1)}, f32[64,8,1,16]{0,3,1,2:T(8,128)}, u32[]{:S(2)}) copy-start(f32[64,8,1,16]{0,3,1,2:T(8,128)} %copy-done.9) | copy-start | bytes 98308
  212.6 36.9 %copy-start.12 = (f32[64,8,1,16]{0,3,1,2:T(8,128)S(1)}, f32[64,8,1,16]{0,3,1,2:T(8,128)}, u32[]{:S(2)}) copy-start(f32[64,8,1,16]{0,3,1,2:T(8,128)} %copy-done.11) | copy-start | bytes 98308
  212.6 36.9 %copy-start.14 = (f32[64,8,1,16]{0,3,1,2:T(8,128)S(1)}, f32[64,8,1,16]{0,3,1,2:T(8,128)}, u32[]{:S(2)}) copy-start(f32[64,8,1,16]{0,3,1,2:T(8,128)} %copy-done.13) | copy-start | bytes 98308
  212.6 42.2 %copy-start = (bf16[8,8,8,16,1,1,16]{6,3,2,1,0,5,4:T(8,128)(2,1)S(1)}, bf16[8,8,8,16,1,1,16]{6,3,2,1,0,5,4:T(8,128)(2,1)}, u32[]{:S(2)}) copy-start(bf16[8,8,8,16,1,1,16]{6,3,2,1,0,5,4:T(8,128)(2,1)} %copy.70) | copy-start | bytes 786436
  212.6 42.2 %copy-start.6 = (bf16[64,32,1,16]{0,3,1,2:T(8,128)(2,1)S(1)}, bf16[64,32,1,16]{0,3,1,2:T(8,128)(2,1)}, u32[]{:S(2)}) copy-start(bf16[64,32,1,16]{0,3,1,2:T(8,128)(2,1)} %copy-done.5) | copy-start | bytes 196612
  249.7 9.1 %collective-permute-start.10 = (bf16[64,32,1,16]{0,3,1,2:T(8,128)(2,1)S(1)}, bf16[64,32,1,16]{0,3,1,2:T(8,128)(2,1)S(1)}, u32[]{:S(2)}, u32[]{:S(2)}) collective-permute-start(bf16[64,32,1,16]{0,3,1,2:T(8,128)(2,1)S(1)} %fusion.37), channel_id=1, source_target_pairs={{0,1},{1,2},{2,3},{3,4},{4,5},{5,6},{6,7},{8,9},{9,10},{10,11},{11... | collective-permute-start | bytes 196616 | tf_op jit(solution)/shard_map/ppermute | solution.py:16
  253.3 8.0 %collective-permute-start.11 = (bf16[64,32,1,16]{0,3,1,2:T(8,128)(2,1)S(1)}, bf16[64,32,1,16]{0,3,1,2:T(8,128)(2,1)S(1)}, u32[]{:S(2)}, u32[]{:S(2)}) collective-permute-start(bf16[64,32,1,16]{0,3,1,2:T(8,128)(2,1)S(1)} %fusion.37), channel_id=1, source_target_pairs={{1,0},{2,1},{3,2},{4,3},{5,4},{6,5},{7,6},{9,8},{10,9},{11,10},{12... | collective-permute-start | bytes 196616 | tf_op jit(solution)/shard_map/ppermute | solution.py:19
  254.8 2.9 copy-start.16
Sparse Core Ops, SparseCore 0:
  258.9 268.1 all-reduce.7
where the time goes:
time: 542 us; the launch traced here: 538 us
  waiting for transfers between devices  264 us (49%)
  blocking collectives  117 us (22%)
  local copies, waits for them, and re-layouts  76.8 us (14%)
  starting transfers between devices  37.6 us (7%)
  matrix products  16.3 us (3%)
  between operations  15.5 us (3%)
  other arithmetic  11.2 us (2%)
    psum x1, waiting for transfers between devices, on_device(): lax.psum((enc_total, dec_total, jnp.einsum('kn,cn->kc', grad_rows, enc_fl...  256 us
    psum x1, blocking collectives, on_device(): lax.psum((enc_total, dec_total, jnp.einsum('kn,cn->kc', grad_rows, enc_fl...  80.2 us
    all_gather x1, blocking collectives, on_device(): enc_grad = lax.all_gather(enc_grad_own, 'wide', axis=1, tiled=True)  36.5 us
    ppermute x6, starting transfers between devices, padded_2(): lax.ppermute(lax.slice_in_dim(block, block.shape[dim] - width, None, axis...  28.3 us
    concatenate x15, local copies, waits for them, and re-layouts, columns(): return jnp.concatenate(pieces, 0)  15.1 us
    unnamed x175, local copies, waits for them, and re-layouts  14.7 us
    slice x17, local copies, waits for them, and re-layouts, columns(): padded[:, first + shift_x:first + shift_x + count, shift_z:shift_z + dept...  11.8 us
  transfers between devices with their start and end apart: 13, of which 4 were waited for; matrix products, arithmetic and copies ran while one was open for 7% of the time, Pallas kernels for 0%

commit v1 on v0

v1 whole, which is shorter than its diff:
```python
import math

import jax
import jax.numpy as jnp
from jax import lax
from jax.experimental import pallas as pl
from jax.experimental.pallas import tpu as pltpu
from jax.sharding import PartitionSpec as P

MESH = pl.DeviceIdType.MESH
BF = jnp.bfloat16
F32 = jnp.float32
NW = 32
NN = 8
RATIO = 8
CH = 64
FCH = 16


def dot_nt(a, b):
    return lax.dot_general(a, b, (((1,), (1,)), ((), ())), preferred_element_type=F32)


def dot_nn(a, b):
    return lax.dot_general(a, b, (((1,), (0,)), ((), ())), preferred_element_type=F32)


def dot_tn(a, b):
    return lax.dot_general(a, b, (((0,), (0,)), ((), ())), preferred_element_type=F32)


def silu_slope(values):
    sigma = jax.nn.sigmoid(values)
    return sigma * (1.0 + values * (1.0 - sigma))


def iota(shape, dim):
    return lax.broadcasted_iota(jnp.int32, shape, dim)


def mult(value, of):
    return pl.multiple_of(value, of)


def shifted_rows(field):
    rows = field.shape[0]
    y = iota(field.shape, 0) % 16
    low = jnp.where(y == 0, 0.0, pltpu.roll(field, 1, 0))
    high = jnp.where(y == 15, 0.0, pltpu.roll(field, rows - 1, 0))
    return jnp.concatenate([low, field, high], axis=1).astype(BF)


def shifted_lanes(field):
    lane = iota(field.shape, 1)
    low = jnp.where(lane == 0, 0.0, pltpu.roll(field, 1, 1))
    high = jnp.where(lane == 127, 0.0, pltpu.roll(field, 127, 1))
    return low, high


def expand(enc):
    rep = jnp.broadcast_to(enc[:, None, :], (16, 8, 64)).reshape(128, 64)
    wide = jnp.concatenate([rep] * 8, axis=1)
    mask = (iota((128, 512), 0) % 8) == (iota((128, 512), 1) // 64)
    return jnp.where(mask, wide, 0.0).astype(BF)


def remote(src, dst, send, recv, target):
    return pltpu.make_async_remote_copy(
        src_ref=src, dst_ref=dst, send_sem=send, recv_sem=recv, device_id=target, device_id_type=MESH
    )


def kernel(
    dark, we, wd, tab, t1, t2, cot,
    gd_out, ge_out, gu_out, gw_out,
    dark_g, de, cot_p, encx, v, dg, gacc, ug, ur, es, eg, ee, encf, ga, gp, gr,
    h1s, h1r, h2s, h2r, h3s, h3r, h4s, h4r,
    dark_ss, dark_rs, cot_ss, cot_rs, ug_ss, ug_rs, e1_ss, e1_rs, e2_ss, e2_rs,
    gp_ss, gp_rs, h1_ss, h1_rs, h2_ss, h2_rs, h3_ss, h3_rs, h4_ss, h4_rs,
):
    w = lax.axis_index("wide")
    n = lax.axis_index("narrow")
    wl, wr = (w + NW - 1) % NW, (w + 1) % NW
    nl, nr = (n + NN - 1) % NN, (n + 1) % NN
    quad = w // 4
    seat = w % 4

    barrier = pltpu.get_barrier_semaphore()

    def greet(target):
        pl.semaphore_signal(barrier, inc=1, device_id=target, device_id_type=MESH)

    @pl.loop(1, NN)
    def _(d):
        greet({"wide": w, "narrow": (n + d) % NN})

    @pl.loop(1, NW)
    def _(d):
        greet({"wide": (w + d) % NW, "narrow": n})

    for a in (wl, wr):
        for b in (nl, nr):
            greet({"wide": a, "narrow": b})

    dark_g[n] = dark[...]
    for i in range(8):
        cot_p[i + 1, 16:144, :] = cot[i]
    zero_plane = jnp.zeros((576, 192), BF)
    for i in (0, 1, 10, 11):
        de[i] = zero_plane

    @pl.loop(2, 10)
    def _(i):
        de[i, 0:32, :] = jnp.zeros((32, 192), BF)
        de[i, 544:576, :] = jnp.zeros((32, 192), BF)

    zero_coarse = jnp.zeros((512, 64), BF)
    eg[0] = zero_coarse
    eg[9] = zero_coarse
    for i in range(3):
        ee[i, 0:16, :] = jnp.zeros((16, 192), BF)
        ee[i, 528:544, :] = jnp.zeros((16, 192), BF)

    pl.semaphore_wait(barrier, NN - 1 + NW - 1 + 4)

    def dark_copy(d):
        return remote(
            dark, dark_g.at[n], dark_ss.at[d], dark_rs.at[d], {"wide": w, "narrow": (n + d) % NN}
        )

    @pl.loop(1, NN)
    def _(d):
        dark_copy(d).start()

    cot_copies = []
    for dx in (-1, 0, 1):
        for dz in (-1, 0, 1):
            if dx == 0 and dz == 0:
                continue
            tw = (wl, w, wr)[dx + 1]
            tn = (nl, n, nr)[dz + 1]
            sx = {-1: (0, 1), 0: (0, 8), 1: (7, 1)}[dx]
            sz = {-1: (0, 16), 0: (0, 128), 1: (112, 16)}[dz]
            tx = {-1: 9, 0: 1, 1: 0}[dx]
            tz = {-1: 144, 0: 16, 1: 0}[dz]
            index = len(cot_copies)
            cot_copies.append(
                remote(
                    cot.at[pl.ds(sx[0], sx[1]), pl.ds(sz[0], sz[1]), :],
                    cot_p.at[pl.ds(tx, sx[1]), pl.ds(tz, sz[1]), :],
                    cot_ss.at[index],
                    cot_rs.at[index],
                    {"wide": tw, "narrow": tn},
                )
            )
    for copy in cot_copies:
        copy.start()

    @pl.loop(1, NN)
    def _(d):
        dark_copy(d).wait_recv()

    @pl.loop(0, NN)
    def _(z):
        de[z + 2, 32:544, :] = shifted_rows(dark_g[z].astype(F32))

    enc_pre_own = None
    for dz in range(3):
        acc = jnp.zeros((48, 64), F32)
        for a in range(3):
            for b in range(3):
                rows = de[n + dz + b, pl.ds(mult((w + a) * 16, 16), 48), :]
                acc = acc + dot_nt(rows, we[3 * a + b])
        if dz == 1:
            enc_pre_own = acc[16:32]
        enc = (acc * jax.nn.sigmoid(acc)).astype(BF).astype(F32)
        z_ok = jnp.logical_and(n + dz - 1 >= 0, n + dz - 1 < NN)
        for dx in range(3):
            x_ok = jnp.logical_and(w + dx - 1 >= 0, w + dx - 1 < NW)
            keep = jnp.where(jnp.logical_and(x_ok, z_ok), 1, 0)
            cell = enc[16 * dx : 16 * dx + 16]
            cell = jnp.where(jnp.full((16, 64), keep, jnp.int32) == 1, cell, 0.0)
            encx[dx * 3 + dz] = expand(cell)

    @pl.loop(0, 12)
    def _(xh):
        i = (xh + 6) % 8
        dx = (xh + 6) // 8
        for dz, first, count, place in ((0, 96, 32, 0), (1, 0, 128, 2), (2, 0, 32, 10)):
            rows = tab[pl.ds(mult(i * 128 + first, 16), count), :]
            up = dot_nt(rows, encx[dx * 3 + dz]).astype(BF).astype(F32)
            low, high = shifted_lanes(up)
            base = xh * 576 + place * 16
            v[pl.ds(mult(base, 16), count), :] = low.astype(BF)
            v[pl.ds(mult(base + 192, 16), count), :] = up.astype(BF)
            v[pl.ds(mult(base + 384, 16), count), :] = high.astype(BF)

    for copy in cot_copies:
        copy.wait_recv()

    @pl.loop(0, 10)
    def _(xh):
        pre = dot_nn(t1[...], v[pl.ds(mult(xh * 576, 16), 1728), :])
        grad = (cot_p[xh].astype(F32) * silu_slope(pre)).astype(BF).astype(F32)
        x_edge = jnp.logical_or(
            jnp.logical_and(w == 0, xh == 0), jnp.logical_and(w == NW - 1, xh == 9)
        )
        z_row = iota((160, 128), 0) // 16
        low_row = jnp.where(n == 0, 0, -1)
        high_row = jnp.where(n == NN - 1, 9, -1)
        edge = jnp.full((160, 128), jnp.where(x_edge, 1, 0), jnp.int32)
        drop = (z_row == low_row) | (z_row == high_row) | (edge == 1)
        grad = jnp.where(drop, 0.0, grad)
        low, high = shifted_lanes(grad)
        base = xh * 480
        dg[pl.ds(mult(base, 16), 160), :] = low.astype(BF)
        dg[pl.ds(mult(base + 160, 16), 160), :] = grad.astype(BF)
        dg[pl.ds(mult(base + 320, 16), 160), :] = high.astype(BF)

    gacc[...] = jnp.zeros((128, 1792), F32)

    @pl.loop(0, 8)
    def _(x):
        rows = dg[pl.ds(mult((x + 1) * 480 + 176, 16), 128), :]
        taps = v[pl.ds(mult((x + 1) * 576, 16), 1728), :]
        gacc[:, 0:1728] += dot_nt(rows, taps)

    total = gacc[0:16, :]
    for z in range(1, 8):
        total = total + pltpu.roll(gacc[16 * z : 16 * z + 16, :], 1792 - 16 * z, 1)
    pieces = [total[:, 192 * i + 16 : 192 * i + 64] for i in range(9)]
    pieces.append(jnp.zeros((16, 80), F32))
    packed = jnp.concatenate(pieces, axis=1)
    for p in range(8):
        h1s[p] = packed[8 * (p // 4) : 8 * (p // 4) + 8, 128 * (p % 4) : 128 * (p % 4) + 128]
    h1r[quad] = h1s[quad]

    def h1_copy(d):
        p = (quad + d) % 8
        return remote(
            h1s.at[p], h1r.at[quad], h1_ss.at[d], h1_rs.at[d], {"wide": p * 4 + seat, "narrow": n}
        )

    @pl.loop(1, 8)
    def _(d):
        h1_copy(d).start()

    @pl.loop(0, 8)
    def _(x):
        back = dot_nn(t2[...], dg[pl.ds(mult(x * 480, 16), 1440), :])
        grad = (cot_p[x + 1, 16:144, :].astype(F32) + back).astype(BF)
        for q in range(4):
            ug[x * 4 + q] = grad[32 * q : 32 * q + 32]

    def ug_copy(d):
        t = (w + d) % NW
        return remote(ug.at[t], ur.at[w], ug_ss.at[d], ug_rs.at[d], {"wide": t, "narrow": n})

    @pl.loop(1, NW)
    def _(d):
        ug_copy(d).start()

    ur[w] = ug[w]

    mixed = dot_tn(ug[...].reshape(1024, 128), tab[...])
    mask = (iota((128, 512), 0) % 8) == (iota((128, 512), 1) // 64)
    mixed = jnp.where(mask, mixed, 0.0)
    folded = mixed[:, 0:64]
    for k in range(1, 8):
        folded = folded + mixed[:, 64 * k : 64 * k + 64]
    enc_grad = jnp.sum(folded.reshape(16, 8, 64), axis=1).astype(BF).astype(F32)
    pre_grad = (enc_grad * silu_slope(enc_pre_own)).astype(BF)
    es[...] = pre_grad
    eg[n + 1, pl.ds(mult(w * 16, 16), 16), :] = pre_grad

    def e1_copy(d):
        return remote(
            es,
            eg.at[n + 1, pl.ds(mult(w * 16, 16), 16), :],
            e1_ss.at[d],
            e1_rs.at[d],
            {"wide": (w + d) % NW, "narrow": n},
        )

    @pl.loop(1, NW)
    def _(d):
        e1_copy(d).start()

    @pl.loop(1, 8)
    def _(d):
        h1_copy(d).wait_recv()

    h2s[...] = jnp.sum(h1r[...], axis=0)
    h2r[seat] = h2s[...]

    def h2_copy(d):
        t = quad * 4 + (seat + d) % 4
        return remote(h2s, h2r.at[seat], h2_ss.at[d], h2_rs.at[d], {"wide": t, "narrow": n})

    @pl.loop(1, 4)
    def _(d):
        h2_copy(d).start()

    acc = jnp.zeros((512, 64), F32)
    for a in range(3):
        for b in range(3):
            acc = acc + dot_nt(de[n + 1 + b, 16 + 16 * a : 528 + 16 * a, :], we[3 * a + b])
    encf[...] = (acc * jax.nn.sigmoid(acc)).astype(BF)

    @pl.loop(1, NW)
    def _(d):
        e1_copy(d).wait_recv()

    def e2_copy(d):
        return remote(
            eg.at[n + 1], eg.at[n + 1], e2_ss.at[d], e2_rs.at[d], {"wide": w, "narrow": (n + d) % NN}
        )

    @pl.loop(1, NN)
    def _(d):
        e2_copy(d).start()

    @pl.loop(1, 4)
    def _(d):
        h2_copy(d).wait_recv()

    h3s[...] = jnp.sum(h2r[...], axis=0)
    h3r[n] = h3s[...]

    def h3_copy(d):
        return remote(
            h3s, h3r.at[n], h3_ss.at[d], h3_rs.at[d], {"wide": w, "narrow": (n + d) % NN}
        )

    @pl.loop(1, NN)
    def _(d):
        h3_copy(d).start()

    @pl.loop(1, NW)
    def _(d):
        ug_copy(d).wait_recv()

    def up_step(x, total):
        cells = encf[pl.ds(mult(x * 16, 16), 16), :].astype(F32)
        return total + dot_nn(ur[x], expand(cells))

    up_total = lax.fori_loop(0, NW, up_step, jnp.zeros((32, 512), F32))
    for p in range(8):
        gp[p] = up_total[16 * (p // 4) : 16 * (p // 4) + 16, 128 * (p % 4) : 128 * (p % 4) + 128]
    gr[n] = gp[n]

    def gp_copy(d):
        t = (n + d) % NN
        return remote(gp.at[t], gr.at[n], gp_ss.at[d], gp_rs.at[d], {"wide": w, "narrow": t})

    @pl.loop(1, NN)
    def _(d):
        gp_copy(d).start()

    @pl.loop(1, NN)
    def _(d):
        h3_copy(d).wait_recv()

    h4s[...] = jnp.sum(h3r[...], axis=0)
    h4r[quad] = h4s[...]

    def h4_copy(d):
        t = ((quad + d) % 8) * 4 + seat
        return remote(h4s, h4r.at[quad], h4_ss.at[d], h4_rs.at[d], {"wide": t, "narrow": n})

    @pl.loop(1, 8)
    def _(d):
        h4_copy(d).start()

    @pl.loop(1, NN)
    def _(d):
        e2_copy(d).wait_recv()

    for b in range(3):
        ee[b, 16:528, :] = shifted_rows(eg[n + b].astype(F32))
    acc = jnp.zeros((512, 64), F32)
    for a in range(3):
        for b in range(3):
            acc = acc + dot_nn(ee[b, 16 * a : 16 * a + 512, :], wd[3 * a + b])
    gd_out[...] = acc

    ga[...] = jnp.zeros((3, 192, 192), F32)

    @pl.loop(0, NN)
    def _(z):
        stack = jnp.concatenate([eg[z + 2], eg[z + 1], eg[z]], axis=1)
        for a in range(3):
            ga[a] += dot_tn(stack, de[z + 2, 16 + 16 * a : 528 + 16 * a, :])

    coarse_scale = 1.0 / 64.0
    for a in range(3):
        for b in range(3):
            for e in range(3):
                ge_out[9 * a + 3 * b + e] = (
                    ga[a, 64 * b : 64 * b + 64, 64 * e : 64 * e + 64] * coarse_scale
                )

    @pl.loop(1, NN)
    def _(d):
        gp_copy(d).wait_recv()

    up_sum = jnp.sum(gr[...], axis=0) * coarse_scale
    gu_out[0] = up_sum[:, 0:64]
    gu_out[1] = up_sum[:, 64:128]

    @pl.loop(1, 8)
    def _(d):
        h4_copy(d).wait_recv()

    fine_scale = 1.0 / math.sqrt(2097152.0)
    for p in range(8):
        gw_out[8 * (p // 4) : 8 * (p // 4) + 8, 128 * (p % 4) : 128 * (p % 4) + 128] = (
            h4r[p] * fine_scale
        )

    for copy in cot_copies:
        copy.wait_send()

    @pl.loop(1, NN)
    def _(d):
        dark_copy(d).wait_send()
        e2_copy(d).wait_send()
        gp_copy(d).wait_send()
        h3_copy(d).wait_send()
        h1_copy(d).wait_send()
        h4_copy(d).wait_send()

    @pl.loop(1, 4)
    def _(d):
        h2_copy(d).wait_send()

    @pl.loop(1, NW)
    def _(d):
        ug_copy(d).wait_send()
        e1_copy(d).wait_send()


def on_device(dark, w_enc, up_weight, w_dec, cotangent):
    dark_q = dark.transpose(1, 2, 3, 0).reshape(512, 64)
    taps = w_enc.reshape(9, 3, CH, CH)
    we = taps.transpose(0, 2, 1, 3).reshape(9, CH, 3 * CH)
    wd = w_enc[::-1].reshape(9, 3 * CH, CH)
    tab = up_weight.reshape(64, 8, FCH, CH).transpose(0, 2, 1, 3).reshape(1024, 512)
    dec = w_dec.reshape(3, 3, 3, FCH, FCH)
    fwd = dec.transpose(3, 0, 2, 1, 4).reshape(FCH, 9, 48)
    t1 = jnp.stack(
        [jnp.pad(fwd, ((0, 0), (0, 0), (16 * z, 144 - 16 * z))) for z in range(10)], 0
    ).reshape(160, 1728)
    bwd = dec[::-1, ::-1, ::-1].transpose(4, 0, 2, 1, 3).reshape(FCH, 9, 48)
    t2 = jnp.stack(
        [jnp.pad(bwd, ((0, 0), (0, 0), (16 * z, 112 - 16 * z))) for z in range(8)], 0
    ).reshape(128, 1440)
    cot = cotangent.transpose(1, 2, 0, 3).reshape(8, 128, 128)
    vmem = pl.BlockSpec(memory_space=pltpu.VMEM)
    dma = pltpu.SemaphoreType.DMA
    gd, ge, gu, gw = pl.pallas_call(
        kernel,
        name="step",
        out_shape=(
            jax.ShapeDtypeStruct((512, 64), F32),
            jax.ShapeDtypeStruct((27, 64, 64), F32),
            jax.ShapeDtypeStruct((2, 16, 64), F32),
            jax.ShapeDtypeStruct((16, 512), F32),
        ),
        in_specs=[vmem] * 7,
        out_specs=(vmem,) * 4,
        scratch_shapes=[
            pltpu.VMEM((8, 512, 64), BF),
            pltpu.VMEM((12, 576, 192), BF),
            pltpu.VMEM((10, 160, 128), BF),
            pltpu.VMEM((9, 128, 512), BF),
            pltpu.VMEM((6912, 128), BF),
            pltpu.VMEM((4800, 128), BF),
            pltpu.VMEM((128, 1792), F32),
            pltpu.VMEM((32, 32, 128), BF),
            pltpu.VMEM((32, 32, 128), BF),
            pltpu.VMEM((16, 64), BF),
            pltpu.VMEM((10, 512, 64), BF),
            pltpu.VMEM((3, 544, 192), BF),
            pltpu.VMEM((512, 64), BF),
            pltpu.VMEM((3, 192, 192), F32),
            pltpu.VMEM((8, 16, 128), F32),
            pltpu.VMEM((8, 16, 128), F32),
            pltpu.VMEM((8, 8, 128), F32),
            pltpu.VMEM((8, 8, 128), F32),
            pltpu.VMEM((8, 128), F32),
            pltpu.VMEM((4, 8, 128), F32),
            pltpu.VMEM((8, 128), F32),
            pltpu.VMEM((8, 8, 128), F32),
            pltpu.VMEM((8, 128), F32),
            pltpu.VMEM((8, 8, 128), F32),
            dma((8,)), dma((8,)), dma((8,)), dma((8,)),
            dma((32,)), dma((32,)), dma((32,)), dma((32,)), dma((8,)), dma((8,)),
            dma((8,)), dma((8,)), dma((8,)), dma((8,)), dma((4,)), dma((4,)),
            dma((8,)), dma((8,)), dma((8,)), dma((8,)),
        ],
        compiler_params=pltpu.CompilerParams(
            collective_id=0, has_side_effects=True, vmem_limit_bytes=60000000
        ),
    )(dark_q, we, wd, tab, t1, t2, cot)
    grad_dark = gd.reshape(32, 1, 16, 64).transpose(3, 0, 1, 2)
    grad_dec = (
        gw[:, :432].reshape(FCH, 3, 3, 3, FCH).transpose(1, 3, 2, 0, 4).reshape(27, FCH, FCH)
    )
    return grad_dark, ge, gu, grad_dec


def solution(mesh):
    in_specs = (P(None, None, "narrow", None), P(), P(), P(), P(None, "wide", "narrow", None))
    out_specs = (P(None, None, "narrow", None), P(), P(("wide", "narrow"), None, None), P())
    return jax.shard_map(
        on_device, mesh=mesh, in_specs=in_specs, out_specs=out_specs, check_vma=False
    )
```

time: 542 us -> 105 us (0.19)
  waiting for transfers between devices: 264 us -> 0 us
  blocking collectives: 117 us -> 0 us
  Pallas kernels: 0 us -> 80.8 us
  local copies, waits for them, and re-layouts: 76.8 us -> 23.3 us
  starting transfers between devices: 37.6 us -> 0 us
  matrix products: 16.3 us -> 0 us
  between operations: 15.5 us -> 0.89 us
  other arithmetic: 11.2 us -> 0 us
    psum x1 -> x0, waiting for transfers between devices: 256 us -> none  [on_device(): lax.psum((enc_total, dec_total, jnp.einsum('kn,cn->kc', grad_rows, enc_fl...]
    pallas_call x0 -> x1, Pallas kernels: none -> 80.8 us  [on_device(): pl.pallas_call(kernel, name='step', out_shape=(jax.ShapeDtypeStruct((512,...]
    psum x1 -> x0, blocking collectives: 80.2 us -> none  [on_device(): lax.psum((enc_total, dec_total, jnp.einsum('kn,cn->kc', grad_rows, enc_fl...]
    ppermute x12 -> x0, starting transfers between devices: 37.6 us -> none  [the longest x6 28.3 us: padded_2(): lax.ppermute(lax.slice_in_dim(block, block.shape[dim] - width, None, axis...]
    all_gather x1 -> x0, blocking collectives: 36.5 us -> none  [on_device(): enc_grad = lax.all_gather(enc_grad_own, 'wide', axis=1, tiled=True)]
    dot_general x24 -> x0, matrix products: 16.3 us -> none  [the longest x12 7.63 us: convolve_blocks(): jnp.einsum('ok,kxzy->oxzy', flat, stacked, preferred_element_type=jnp.flo...]
    concatenate x16 -> x0, local copies, waits for them, and re-layouts: 15.1 us -> none  [the longest x15 15.1 us: columns(): return jnp.concatenate(pieces, 0)]
    slice x21 -> x0, local copies, waits for them, and re-layouts: 13.1 us -> none  [the longest x17 11.8 us: columns(): padded[:, first + shift_x:first + shift_x + count, shift_z:shift_z + dept...]
  transfers between devices with their start and end apart: 13 -> 0, of which waited for: 4 -> 0; matrix products, arithmetic and copies ran while one was open for 7% -> 0% of each run, Pallas kernels for 0% -> 0%
where the time goes in v1:
time: 105 us
  Pallas kernels  80.8 us (77%)
  local copies, waits for them, and re-layouts  23.3 us (22%)
    pallas_call x1, Pallas kernels, on_device(): pl.pallas_call(kernel, name='step', out_shape=(jax.ShapeDtypeStruct((512,...  80.8 us
    unnamed x32, local copies, waits for them, and re-layouts  8.29 us
    transpose x1, local copies, waits for them, and re-layouts, on_device(): up_weight.reshape(64, 8, FCH, CH).transpose(0, 2, 1, 3).reshape(1024, 512)  2.13 us

profile of v1, /device:TPU:1, one launch (start us, length us, event | category | flops | bytes accessed | tf_op | source)
XLA Modules:
  0.0 105.0 jit_solution(97691492016827562)
XLA Ops:
  0.6 0.0 copy-start
  0.6 1.3 %copy.16 = bf16[9,3,64,64]{2,3,1,0:T(8,128)(2,1)S(1)} copy(bf16[9,3,64,64]{3,2,1,0:T(8,128)(2,1)} %bitcast.69) | data formatting | bytes 442368 | tf_op jit(solution)/shard_map/reshape | solution.py:445
  2.0 0.9 copy.25.we
  2.9 1.8 %rev.6 = bf16[27,64,64]{2,1,0:T(8,128)(2,1)} reverse(bf16[27,64,64]{2,1,0:T(8,128)(2,1)} %param.6), dimensions={0} | reverse | bytes 442368 | tf_op jit(solution)/shard_map/rev | solution.py:447
  4.7 0.0 copy-done
  4.7 2.9 %copy.17 = bf16[512,16,64]{2,1,0:T(8,128)(2,1)} copy(bf16[512,16,64]{0,2,1:T(8,128)(2,1)S(1)} %copy-done) | data formatting | bytes 2097152 | tf_op args[2]
  7.6 2.1 %copy.18 = bf16[64,16,8,64]{3,2,1,0:T(8,128)(2,1)S(1)} copy(bf16[64,16,8,64]{3,1,2,0:T(8,128)(2,1)} %bitcast.68) | data formatting | bytes 2097152 | tf_op jit(solution)/shard_map/transpose | solution.py:448
  9.7 0.0 copy-start.3
  9.7 2.1 %reshape.58.tab = bf16[1024,512]{1,0:T(8,128)(2,1)} reshape(bf16[64,16,8,64]{3,2,1,0:T(8,128)(2,1)S(1)} %copy.18) | data formatting | bytes 2097152 | tf_op jit(solution)/shard_map/reshape | solution.py:448
  11.8 0.0 copy-done.3
  11.8 0.2 copy.19
  12.0 0.1 copy.20
  12.1 0.1 reshape.60
  12.2 0.1 bitcast_dynamic-update-slice_fusion.16
  12.3 0.1 bitcast_dynamic-update-slice_fusion.15
  12.4 0.1 bitcast_dynamic-update-slice_fusion.14
  12.5 0.1 bitcast_dynamic-update-slice_fusion.13
  12.6 0.1 bitcast_dynamic-update-slice_fusion.12
  12.7 0.1 bitcast_dynamic-update-slice_fusion.11
  12.8 0.1 bitcast_dynamic-update-slice_fusion.10
  12.9 0.1 bitcast_dynamic-update-slice_fusion.8
  13.0 0.4 copy.21
  13.4 1.7 %reshape.61.t1 = bf16[160,1728]{1,0:T(8,128)(2,1)} reshape(bf16[10,16,9,192]{3,2,1,0:T(8,128)(2,1)S(1)} %copy.21) | data formatting | bytes 1105920 | tf_op jit(solution)/shard_map/reshape | solution.py:453
  15.1 0.1 copy.22
  15.3 0.0 copy-start.2
  15.3 0.1 reshape.62
  15.4 0.1 bitcast_dynamic-update-slice_fusion.6
  15.5 0.1 bitcast_dynamic-update-slice_fusion.5
  15.6 0.1 bitcast_dynamic-update-slice_fusion.4
  15.7 0.1 bitcast_dynamic-update-slice_fusion.3
  15.8 0.1 bitcast_dynamic-update-slice_fusion.2
  15.9 0.1 bitcast_dynamic-update-slice_fusion.1
  16.0 0.1 bitcast_dynamic-update-slice_fusion
  16.1 0.3 copy.23
  16.4 1.8 %reshape.63.t2 = bf16[128,1440]{1,0:T(8,128)(2,1)} reshape(bf16[8,16,9,160]{3,2,1,0:T(8,128)(2,1)S(1)} %copy.23) | data formatting | bytes 737280 | tf_op jit(solution)/shard_map/reshape | solution.py:457
  18.2 0.0 copy-done.2
  18.2 0.9 copy.24
  19.1 80.8 %step.1 = (f32[512,64]{1,0:T(8,128)}, f32[27,64,64]{2,1,0:T(8,128)}, f32[2,16,64]{2,1,0:T(8,128)}, f32[16,512]{1,0:T(8,128)}) custom-call(bf16[512,64]{1,0:T(8,128)(2,1)} %bitcast.79, bf16[9,64,192]{2,1,0:T(8,128)(2,1)} %copy.25.we, bf16[9,192,64]{2,1,0:T(8,128)(2,1)} %bitcast.70, bf16[1024,512]{1,0:T(8,128)(2,1)} %reshape.58.tab, ...), custom_call_target="tpu_custom_call" | custom-call | tf_op jit(solution)/shard_map/step/pallas_call | solution.py:461
  99.9 0.0 copy-start.1
  99.9 0.0 copy-start.4
  99.9 1.0 reshape.66
  100.9 0.8 copy.28
  101.8 1.7 %copy.48 = f32[64,32,1,16]{0,3,2,1:T(8,128)} copy(f32[64,32,1,16]{0,3,2,1:T(8,128)} %bitcast.78) | data formatting | bytes 262144
  103.4 0.0 copy-done.1
  103.4 0.9 copy.49
  104.3 0.0 copy-done.4
  104.3 0.6 copy.50
  (5 shorter events, 0.1 us)
Async XLA Ops:
  0.6 4.1 %copy-start = (bf16[512,16,64]{0,2,1:T(8,128)(2,1)S(1)}, bf16[512,16,64]{0,2,1:T(8,128)(2,1)}, u32[]{:S(2)}) copy-start(bf16[512,16,64]{0,2,1:T(8,128)(2,1)} %param.7) | copy-start | bytes 3145732
  9.7 2.1 %copy-start.3 = (bf16[27,16,16]{0,2,1:T(8,128)(2,1)S(1)}, bf16[27,16,16]{0,2,1:T(8,128)(2,1)}, u32[]{:S(2)}) copy-start(bf16[27,16,16]{0,2,1:T(8,128)(2,1)} %param.8) | copy-start | bytes 41476
  15.3 3.0 %copy-start.2 = (bf16[16,8,8,128]{3,2,1,0:T(8,128)(2,1)S(1)}, bf16[16,8,8,128]{3,2,1,0:T(8,128)(2,1)}, u32[]{:S(2)}) copy-start(bf16[16,8,8,128]{3,2,1,0:T(8,128)(2,1)} %param.9) | copy-start | bytes 786436
  99.9 3.6 %copy-start.1 = (f32[27,64,64]{2,1,0:T(8,128)S(1)}, f32[27,64,64]{2,1,0:T(8,128)}, u32[]{:S(2)}) copy-start(f32[27,64,64]{2,1,0:T(8,128)} %get-tuple-element.21) | copy-start | bytes 1327108
  99.9 4.5 %copy-start.4 = (f32[2,16,64]{2,1,0:T(8,128)S(1)}, f32[2,16,64]{2,1,0:T(8,128)}, u32[]{:S(2)}) copy-start(f32[2,16,64]{2,1,0:T(8,128)} %get-tuple-element.22) | copy-start | bytes 24580

commit v2 on v1

--- a/solution.py
+++ b/solution.py
@@ -70,12 +70,39 @@
     )
 
 
+class Exchange:
+    def __init__(self, copy, count, pending):
+        self.copy = copy
+        self.count = count
+        self.pending = pending
+        self.landed = False
+
+    def each(self, act):
+        @pl.loop(1, self.count)
+        def _(d):
+            act(self.copy(d))
+
+    def start(self):
+        self.pending.append(self)
+        self.each(lambda c: c.start())
+
+    def wait_recv(self):
+        self.landed = True
+        self.each(lambda c: c.wait_recv())
+
+    def finish(self):
+        if not self.landed:
+            self.wait_recv()
+        self.each(lambda c: c.wait_send())
+
+
 def kernel(
-    dark, we, wd, tab, t1, t2, cot,
+    dark, wenc, uw, wdec, wdec_t, cot,
     gd_out, ge_out, gu_out, gw_out,
-    dark_g, de, cot_p, encx, v, dg, gacc, ug, ur, es, eg, ee, encf, ga, gp, gr,
+    rows_f, cot_f, we, wd, tab, t1, t2, cot_o,
+    dark_pad, dark_w, dew, dark_p, de, e1r, eg_p, cot_p, encx, v, dg, gacc, ug, ur, es, eg, ee, encf, ga, gp, gr,
     h1s, h1r, h2s, h2r, h3s, h3r, h4s, h4r,
-    dark_ss, dark_rs, cot_ss, cot_rs, ug_ss, ug_rs, e1_ss, e1_rs, e2_ss, e2_rs,
+    win_ss, win_rs, dark_ss, dark_rs, dr_ss, dr_rs, er_ss, er_rs, cot_ss, cot_rs, ug_ss, ug_rs, e1_ss, e1_rs, e2_ss, e2_rs,
     gp_ss, gp_rs, h1_ss, h1_rs, h2_ss, h2_rs, h3_ss, h3_rs, h4_ss, h4_rs,
 ):
     w = lax.axis_index("wide")
@@ -84,6 +111,17 @@
     nl, nr = (n + NN - 1) % NN, (n + 1) % NN
     quad = w // 4
     seat = w % 4
+    pending = []
+    cot_copies = []
+    win_copies = []
+
+    def finish():
+        for exchange in pending:
+            exchange.finish()
+        for copy in cot_copies:
+            copy.wait_send()
+        for copy in win_copies:
+            copy.wait_send()
 
     barrier = pltpu.get_barrier_semaphore()
 
@@ -94,25 +132,38 @@
     def _(d):
         greet({"wide": w, "narrow": (n + d) % NN})
 
+    for a in (wl, wr):
+        for b in (nl, nr):
+            greet({"wide": a, "narrow": b})
+
     @pl.loop(1, NW)
     def _(d):
         greet({"wide": (w + d) % NW, "narrow": n})
 
-    for a in (wl, wr):
-        for b in (nl, nr):
-            greet({"wide": a, "narrow": b})
-
-    dark_g[n] = dark[...]
-    for i in range(8):
-        cot_p[i + 1, 16:144, :] = cot[i]
-    zero_plane = jnp.zeros((576, 192), BF)
+    cot_f[...] = cot[...].astype(F32)
+
+    @pl.loop(0, 8)
+    def _(x):
+        for z in range(8):
+            rows = cot_f[pl.ds(x * 8 + z, 16, stride=64), :].astype(BF)
+            cot_o[x, 16 * z : 16 * z + 16, :] = rows
+            cot_p[x + 1, 16 * z + 16 : 16 * z + 32, :] = rows
+
+    core = w % 2
+    mate = w + 1 - 2 * core
+    dark_pad[0:32, :] = jnp.zeros((32, 64), BF)
+    dark_pad[32:544, :] = dark[...]
+    dark_pad[544:576, :] = jnp.zeros((32, 64), BF)
+    pair = dark[...].reshape(16, 32, 64)
+    dark_p[n] = jnp.concatenate([pair[:, 0:16], pair[:, 16:32]], axis=2).reshape(256, 128)
+    dark_w[2] = dark_pad[pl.ds(mult(w * 16, 16), 80), :]
     for i in (0, 1, 10, 11):
-        de[i] = zero_plane
+        de[i] = jnp.zeros((544, 192), BF)
 
     @pl.loop(2, 10)
     def _(i):
-        de[i, 0:32, :] = jnp.zeros((32, 192), BF)
-        de[i, 544:576, :] = jnp.zeros((32, 192), BF)
+        de[i, 0:16, :] = jnp.zeros((16, 192), BF)
+        de[i, 528:544, :] = jnp.zeros((16, 192), BF)
 
     zero_coarse = jnp.zeros((512, 64), BF)
     eg[0] = zero_coarse
@@ -121,18 +172,43 @@
         ee[i, 0:16, :] = jnp.zeros((16, 192), BF)
         ee[i, 528:544, :] = jnp.zeros((16, 192), BF)
 
+    for i in range(9):
+        we[i] = jnp.concatenate([wenc[3 * i + e] for e in range(3)], axis=1)
+        for e in range(3):
+            wd[i, 64 * e : 64 * e + 64, :] = wenc[26 - 3 * i - e]
+
+    def spread(get, block, count, out):
+        zeros = jnp.zeros((16, block - 48), F32)
+        parts = []
+        for a in range(3):
+            for e in range(3):
+                parts += [get(a, b, e).astype(F32) for b in range(3)] + [zeros]
+        pad = -9 * block % 128
+        if pad:
+            parts.append(jnp.zeros((16, pad), F32))
+        base = jnp.concatenate(parts, axis=1)
+        for z in range(count):
+            row = base if z == 0 else pltpu.roll(base, 16 * z, 1)
+            out[16 * z : 16 * z + 16, :] = row[:, 0 : 9 * block].astype(BF)
+
+    spread(lambda a, b, e: wdec[9 * a + 3 * b + e], 192, 10, t1)
+    spread(lambda a, b, e: wdec_t[26 - (9 * a + 3 * b + e)], 160, 8, t2)
+
     pl.semaphore_wait(barrier, NN - 1 + NW - 1 + 4)
 
-    def dark_copy(d):
-        return remote(
-            dark, dark_g.at[n], dark_ss.at[d], dark_rs.at[d], {"wide": w, "narrow": (n + d) % NN}
+    for index, dz in enumerate((1, -1, 2, -2)):
+        win_copies.append(
+            remote(
+                dark_pad.at[pl.ds(mult(w * 16, 16), 80), :],
+                dark_w.at[2 - dz],
+                win_ss.at[index],
+                win_rs.at[index],
+                {"wide": w, "narrow": (n + dz + NN) % NN},
+            )
         )
-
-    @pl.loop(1, NN)
-    def _(d):
-        dark_copy(d).start()
-
-    cot_copies = []
+    for copy in win_copies:
+        copy.start()
+
     for dx in (-1, 0, 1):
         for dz in (-1, 0, 1):
             if dx == 0 and dz == 0:
@@ -146,7 +222,7 @@
             index = len(cot_copies)
             cot_copies.append(
                 remote(
-                    cot.at[pl.ds(sx[0], sx[1]), pl.ds(sz[0], sz[1]), :],
+                    cot_o.at[pl.ds(sx[0], sx[1]), pl.ds(sz[0], sz[1]), :],
                     cot_p.at[pl.ds(tx, sx[1]), pl.ds(tz, sz[1]), :],
                     cot_ss.at[index],
                     cot_rs.at[index],
@@ -155,30 +231,47 @@
             )
     for copy in cot_copies:
         copy.start()
-
-    @pl.loop(1, NN)
-    def _(d):
-        dark_copy(d).wait_recv()
-
-    @pl.loop(0, NN)
-    def _(z):
-        de[z + 2, 32:544, :] = shifted_rows(dark_g[z].astype(F32))
-
-    enc_pre_own = None
+    half = pl.ds(mult(core * 128, 128), 128)
+
+    def dark_copy(d):
+        part = dark_p.at[n, half, :]
+        return remote(
+            part, part, dark_ss.at[d], dark_rs.at[d], {"wide": w, "narrow": (n + d) % NN}
+        )
+
+    dark_x = Exchange(dark_copy, NN, pending)
+    dark_x.start()
+
+    @pl.loop(0, 16)
+    def _(o):
+        rows_f[pl.ds(mult(o * 512, 512), 512), 0:64] = uw[o].astype(F32).T
+
+    @pl.loop(0, 64)
+    def _(ij):
+        parts = [rows_f[pl.ds(ij * 8 + k, 16, stride=512), :][:, 0:64] for k in range(8)]
+        tab[pl.ds(mult(ij * 16, 16), 16), :] = jnp.concatenate(parts, axis=1).astype(BF)
+
+    for copy in win_copies:
+        copy.wait_recv()
+    for i in range(5):
+        plane = n + i - 2
+        inside = jnp.where(jnp.logical_and(plane >= 0, plane < NN), 1, 0)
+        field = jnp.where(jnp.full((80, 64), inside, jnp.int32) == 1, dark_w[i].astype(F32), 0.0)
+        dew[i] = shifted_rows(field)
+
+    acc = jnp.zeros((144, 64), F32)
+    for a in range(3):
+        for b in range(3):
+            rows = jnp.concatenate([dew[dz + b, 16 * a : 16 * a + 48, :] for dz in range(3)], axis=0)
+            acc = acc + dot_nt(rows, we[3 * a + b])
+    enc_pre_own = acc[64:80]
+    enc = (acc * jax.nn.sigmoid(acc)).astype(BF).astype(F32)
     for dz in range(3):
-        acc = jnp.zeros((48, 64), F32)
-        for a in range(3):
-            for b in range(3):
-                rows = de[n + dz + b, pl.ds(mult((w + a) * 16, 16), 48), :]
-                acc = acc + dot_nt(rows, we[3 * a + b])
-        if dz == 1:
-            enc_pre_own = acc[16:32]
-        enc = (acc * jax.nn.sigmoid(acc)).astype(BF).astype(F32)
         z_ok = jnp.logical_and(n + dz - 1 >= 0, n + dz - 1 < NN)
         for dx in range(3):
             x_ok = jnp.logical_and(w + dx - 1 >= 0, w + dx - 1 < NW)
             keep = jnp.where(jnp.logical_and(x_ok, z_ok), 1, 0)
-            cell = enc[16 * dx : 16 * dx + 16]
+            cell = enc[48 * dz + 16 * dx : 48 * dz + 16 * dx + 16]
             cell = jnp.where(jnp.full((16, 64), keep, jnp.int32) == 1, cell, 0.0)
             encx[dx * 3 + dz] = expand(cell)
 
@@ -195,6 +288,23 @@
             v[pl.ds(mult(base + 192, 16), count), :] = up.astype(BF)
             v[pl.ds(mult(base + 384, 16), count), :] = high.astype(BF)
 
+    def relay(buffer, exchange, sends, lands):
+        def copy(d):
+            part = buffer.at[(n + NN - d) % NN, half, :]
+            return remote(part, part, sends.at[d], lands.at[d], {"wide": mate, "narrow": n})
+
+        passed = Exchange(copy, NN, pending)
+        pending.append(passed)
+        exchange.landed = True
+
+        @pl.loop(1, NN)
+        def _(d):
+            exchange.copy(d).wait_recv()
+            copy(d).start()
+
+        return passed
+
+    dark_r = relay(dark_p, dark_x, dr_ss, dr_rs)
     for copy in cot_copies:
         copy.wait_recv()
 
@@ -241,9 +351,8 @@
             h1s.at[p], h1r.at[quad], h1_ss.at[d], h1_rs.at[d], {"wide": p * 4 + seat, "narrow": n}
         )
 
-    @pl.loop(1, 8)
-    def _(d):
-        h1_copy(d).start()
+    h1_x = Exchange(h1_copy, 8, pending)
+    h1_x.start()
 
     @pl.loop(0, 8)
     def _(x):
@@ -251,16 +360,6 @@
         grad = (cot_p[x + 1, 16:144, :].astype(F32) + back).astype(BF)
         for q in range(4):
             ug[x * 4 + q] = grad[32 * q : 32 * q + 32]
-
-    def ug_copy(d):
-        t = (w + d) % NW
-        return remote(ug.at[t], ur.at[w], ug_ss.at[d], ug_rs.at[d], {"wide": t, "narrow": n})
-
-    @pl.loop(1, NW)
-    def _(d):
-        ug_copy(d).start()
-
-    ur[w] = ug[w]
 
     mixed = dot_tn(ug[...].reshape(1024, 128), tab[...])
     mask = (iota((128, 512), 0) % 8) == (iota((128, 512), 1) // 64)
@@ -269,26 +368,32 @@
     for k in range(1, 8):
         folded = folded + mixed[:, 64 * k : 64 * k + 64]
     enc_grad = jnp.sum(folded.reshape(16, 8, 64), axis=1).astype(BF).astype(F32)
-    pre_grad = (enc_grad * silu_slope(enc_pre_own)).astype(BF)
-    es[...] = pre_grad
-    eg[n + 1, pl.ds(mult(w * 16, 16), 16), :] = pre_grad
+    pre_grad = (enc_grad * silu_slope(enc_pre_own)).astype(BF).astype(F32)
+    zero_half = jnp.zeros((16, 64), F32)
+    even = jnp.concatenate([pre_grad, zero_half], axis=1)
+    odd = jnp.concatenate([zero_half, pre_grad], axis=1)
+    tile = jnp.where(jnp.full((16, 128), core, jnp.int32) == 0, even, odd).astype(BF)
+    es[...] = tile
+    e1r[w] = tile
 
     def e1_copy(d):
         return remote(
-            es,
-            eg.at[n + 1, pl.ds(mult(w * 16, 16), 16), :],
-            e1_ss.at[d],
-            e1_rs.at[d],
-            {"wide": (w + d) % NW, "narrow": n},
+            es, e1r.at[w], e1_ss.at[d], e1_rs.at[d], {"wide": (w + d) % NW, "narrow": n}
         )
 
-    @pl.loop(1, NW)
-    def _(d):
-        e1_copy(d).start()
-
-    @pl.loop(1, 8)
-    def _(d):
-        h1_copy(d).wait_recv()
+    e1_x = Exchange(e1_copy, NW, pending)
+    e1_x.start()
+
+    def ug_copy(d):
+        t = (w + d) % NW
+        return remote(ug.at[t], ur.at[w], ug_ss.at[d], ug_rs.at[d], {"wide": t, "narrow": n})
+
+    ug_x = Exchange(ug_copy, NW, pending)
+    ug_x.start()
+
+    ur[w] = ug[w]
+
+    h1_x.wait_recv()
 
     h2s[...] = jnp.sum(h1r[...], axis=0)
     h2r[seat] = h2s[...]
@@ -297,32 +402,40 @@
         t = quad * 4 + (seat + d) % 4
         return remote(h2s, h2r.at[seat], h2_ss.at[d], h2_rs.at[d], {"wide": t, "narrow": n})
 
-    @pl.loop(1, 4)
-    def _(d):
-        h2_copy(d).start()
+    h2_x = Exchange(h2_copy, 4, pending)
+    h2_x.start()
+
+    dark_r.wait_recv()
+
+    def unpack(plane):
+        both = plane.reshape(16, 16, 128)
+        return jnp.stack([both[:, :, 0:64], both[:, :, 64:128]], axis=1).reshape(512, 64)
+
+    @pl.loop(0, NN)
+    def _(z):
+        de[z + 2, 16:528, :] = shifted_rows(unpack(dark_p[z].astype(F32)))
 
     acc = jnp.zeros((512, 64), F32)
     for a in range(3):
         for b in range(3):
-            acc = acc + dot_nt(de[n + 1 + b, 16 + 16 * a : 528 + 16 * a, :], we[3 * a + b])
+            acc = acc + dot_nt(de[n + 1 + b, 16 * a : 512 + 16 * a, :], we[3 * a + b])
     encf[...] = (acc * jax.nn.sigmoid(acc)).astype(BF)
 
-    @pl.loop(1, NW)
-    def _(d):
-        e1_copy(d).wait_recv()
+    e1_x.wait_recv()
+
+    for m in range(16):
+        eg_p[n, 16 * m : 16 * m + 16, :] = (
+            e1r[2 * m].astype(F32) + e1r[2 * m + 1].astype(F32)
+        ).astype(BF)
 
     def e2_copy(d):
-        return remote(
-            eg.at[n + 1], eg.at[n + 1], e2_ss.at[d], e2_rs.at[d], {"wide": w, "narrow": (n + d) % NN}
-        )
-
-    @pl.loop(1, NN)
-    def _(d):
-        e2_copy(d).start()
-
-    @pl.loop(1, 4)
-    def _(d):
-        h2_copy(d).wait_recv()
+        part = eg_p.at[n, half, :]
+        return remote(part, part, e2_ss.at[d], e2_rs.at[d], {"wide": w, "narrow": (n + d) % NN})
+
+    e2_x = Exchange(e2_copy, NN, pending)
+    e2_x.start()
+
+    h2_x.wait_recv()
 
     h3s[...] = jnp.sum(h2r[...], axis=0)
     h3r[n] = h3s[...]
@@ -332,13 +445,10 @@
             h3s, h3r.at[n], h3_ss.at[d], h3_rs.at[d], {"wide": w, "narrow": (n + d) % NN}
         )
 
-    @pl.loop(1, NN)
-    def _(d):
-        h3_copy(d).start()
-
-    @pl.loop(1, NW)
-    def _(d):
-        ug_copy(d).wait_recv()
+    h3_x = Exchange(h3_copy, NN, pending)
+    h3_x.start()
+
+    ug_x.wait_recv()
 
     def up_step(x, total):
         cells = encf[pl.ds(mult(x * 16, 16), 16), :].astype(F32)
@@ -353,13 +463,10 @@
         t = (n + d) % NN
         return remote(gp.at[t], gr.at[n], gp_ss.at[d], gp_rs.at[d], {"wide": w, "narrow": t})
 
-    @pl.loop(1, NN)
-    def _(d):
-        gp_copy(d).start()
-
-    @pl.loop(1, NN)
-    def _(d):
-        h3_copy(d).wait_recv()
+    gp_x = Exchange(gp_copy, NN, pending)
+    gp_x.start()
+
+    h3_x.wait_recv()
 
     h4s[...] = jnp.sum(h3r[...], axis=0)
     h4r[quad] = h4s[...]
@@ -368,13 +475,16 @@
         t = ((quad + d) % 8) * 4 + seat
         return remote(h4s, h4r.at[quad], h4_ss.at[d], h4_rs.at[d], {"wide": t, "narrow": n})
 
-    @pl.loop(1, 8)
-    def _(d):
-        h4_copy(d).start()
-
-    @pl.loop(1, NN)
-    def _(d):
-        e2_copy(d).wait_recv()
+    h4_x = Exchange(h4_copy, 8, pending)
+    h4_x.start()
+
+    eg_r = relay(eg_p, e2_x, er_ss, er_rs)
+    eg_r.wait_recv()
+
+    @pl.loop(0, NN)
+    def _(z):
+        eg[z + 1] = unpack(eg_p[z].astype(F32)).astype(BF)
+
 
     for b in range(3):
         ee[b, 16:528, :] = shifted_rows(eg[n + b].astype(F32))
@@ -390,7 +500,7 @@
     def _(z):
         stack = jnp.concatenate([eg[z + 2], eg[z + 1], eg[z]], axis=1)
         for a in range(3):
-            ga[a] += dot_tn(stack, de[z + 2, 16 + 16 * a : 528 + 16 * a, :])
+            ga[a] += dot_tn(stack, de[z + 2, 16 * a : 512 + 16 * a, :])
 
     coarse_scale = 1.0 / 64.0
     for a in range(3):
@@ -400,62 +510,31 @@
                     ga[a, 64 * b : 64 * b + 64, 64 * e : 64 * e + 64] * coarse_scale
                 )
 
-    @pl.loop(1, NN)
-    def _(d):
-        gp_copy(d).wait_recv()
+    gp_x.wait_recv()
 
     up_sum = jnp.sum(gr[...], axis=0) * coarse_scale
     gu_out[0] = up_sum[:, 0:64]
     gu_out[1] = up_sum[:, 64:128]
 
-    @pl.loop(1, 8)
-    def _(d):
-        h4_copy(d).wait_recv()
+    h4_x.wait_recv()
 
     fine_scale = 1.0 / math.sqrt(2097152.0)
-    for p in range(8):
-        gw_out[8 * (p // 4) : 8 * (p // 4) + 8, 128 * (p % 4) : 128 * (p % 4) + 128] = (
-            h4r[p] * fine_scale
-        )
-
-    for copy in cot_copies:
-        copy.wait_send()
-
-    @pl.loop(1, NN)
-    def _(d):
-        dark_copy(d).wait_send()
-        e2_copy(d).wait_send()
-        gp_copy(d).wait_send()
-        h3_copy(d).wait_send()
-        h1_copy(d).wait_send()
-        h4_copy(d).wait_send()
-
-    @pl.loop(1, 4)
-    def _(d):
-        h2_copy(d).wait_send()
-
-    @pl.loop(1, NW)
-    def _(d):
-        ug_copy(d).wait_send()
-        e1_copy(d).wait_send()
+    top = jnp.concatenate([h4r[p] for p in range(4)], axis=1)
+    low = jnp.concatenate([h4r[p] for p in range(4, 8)], axis=1)
+    dec = jnp.concatenate([top, low], axis=0) * fine_scale
+    for a in range(3):
+        for b in range(3):
+            for e in range(3):
+                place = 144 * a + 48 * e + 16 * b
+                gw_out[9 * a + 3 * b + e] = dec[:, place : place + 16]
+
+    finish()
 
 
 def on_device(dark, w_enc, up_weight, w_dec, cotangent):
     dark_q = dark.transpose(1, 2, 3, 0).reshape(512, 64)
-    taps = w_enc.reshape(9, 3, CH, CH)
-    we = taps.transpose(0, 2, 1, 3).reshape(9, CH, 3 * CH)
-    wd = w_enc[::-1].reshape(9, 3 * CH, CH)
-    tab = up_weight.reshape(64, 8, FCH, CH).transpose(0, 2, 1, 3).reshape(1024, 512)
-    dec = w_dec.reshape(3, 3, 3, FCH, FCH)
-    fwd = dec.transpose(3, 0, 2, 1, 4).reshape(FCH, 9, 48)
-    t1 = jnp.stack(
-        [jnp.pad(fwd, ((0, 0), (0, 0), (16 * z, 144 - 16 * z))) for z in range(10)], 0
-    ).reshape(160, 1728)
-    bwd = dec[::-1, ::-1, ::-1].transpose(4, 0, 2, 1, 3).reshape(FCH, 9, 48)
-    t2 = jnp.stack(
-        [jnp.pad(bwd, ((0, 0), (0, 0), (16 * z, 112 - 16 * z))) for z in range(8)], 0
-    ).reshape(128, 1440)
-    cot = cotangent.transpose(1, 2, 0, 3).reshape(8, 128, 128)
+    up_rows = up_weight.transpose(1, 2, 0)
+    cot = cotangent.reshape(1024, 128)
     vmem = pl.BlockSpec(memory_space=pltpu.VMEM)
     dma = pltpu.SemaphoreType.DMA
     gd, ge, gu, gw = pl.pallas_call(
@@ -465,13 +544,26 @@
             jax.ShapeDtypeStruct((512, 64), F32),
             jax.ShapeDtypeStruct((27, 64, 64), F32),
             jax.ShapeDtypeStruct((2, 16, 64), F32),
-            jax.ShapeDtypeStruct((16, 512), F32),
+            jax.ShapeDtypeStruct((27, 16, 16), F32),
         ),
-        in_specs=[vmem] * 7,
+        in_specs=[vmem] * 6,
         out_specs=(vmem,) * 4,
         scratch_shapes=[
-            pltpu.VMEM((8, 512, 64), BF),
-            pltpu.VMEM((12, 576, 192), BF),
+            pltpu.VMEM((8192, 128), F32),
+            pltpu.VMEM((1024, 128), F32),
+            pltpu.VMEM((9, 64, 192), BF),
+            pltpu.VMEM((9, 192, 64), BF),
+            pltpu.VMEM((1024, 512), BF),
+            pltpu.VMEM((160, 1728), BF),
+            pltpu.VMEM((128, 1440), BF),
+            pltpu.VMEM((8, 128, 128), BF),
+            pltpu.VMEM((576, 64), BF),
+            pltpu.VMEM((5, 80, 64), BF),
+            pltpu.VMEM((5, 80, 192), BF),
+            pltpu.VMEM((8, 256, 128), BF),
+            pltpu.VMEM((12, 544, 192), BF),
+            pltpu.VMEM((32, 16, 128), BF),
+            pltpu.VMEM((8, 256, 128), BF),
             pltpu.VMEM((10, 160, 128), BF),
             pltpu.VMEM((9, 128, 512), BF),
             pltpu.VMEM((6912, 128), BF),
@@ -479,7 +571,7 @@
             pltpu.VMEM((128, 1792), F32),
             pltpu.VMEM((32, 32, 128), BF),
             pltpu.VMEM((32, 32, 128), BF),
-            pltpu.VMEM((16, 64), BF),
+            pltpu.VMEM((16, 128), BF),
             pltpu.VMEM((10, 512, 64), BF),
             pltpu.VMEM((3, 544, 192), BF),
             pltpu.VMEM((512, 64), BF),
@@ -494,7 +586,8 @@
             pltpu.VMEM((8, 8, 128), F32),
             pltpu.VMEM((8, 128), F32),
             pltpu.VMEM((8, 8, 128), F32),
-            dma((8,)), dma((8,)), dma((8,)), dma((8,)),
+            dma((4,)), dma((4,)), dma((8,)), dma((8,)), dma((8,)), dma((8,)), dma((8,)), dma((8,)),
+            dma((8,)), dma((8,)),
             dma((32,)), dma((32,)), dma((32,)), dma((32,)), dma((8,)), dma((8,)),
             dma((8,)), dma((8,)), dma((8,)), dma((8,)), dma((4,)), dma((4,)),
             dma((8,)), dma((8,)), dma((8,)), dma((8,)),
@@ -502,12 +595,9 @@
         compiler_params=pltpu.CompilerParams(
             collective_id=0, has_side_effects=True, vmem_limit_bytes=60000000
         ),
-    )(dark_q, we, wd, tab, t1, t2, cot)
+    )(dark_q, w_enc, up_rows, w_dec, w_dec.transpose(0, 2, 1), cot)
     grad_dark = gd.reshape(32, 1, 16, 64).transpose(3, 0, 1, 2)
-    grad_dec = (
-        gw[:, :432].reshape(FCH, 3, 3, 3, FCH).transpose(1, 3, 2, 0, 4).reshape(27, FCH, FCH)
-    )
-    return grad_dark, ge, gu, grad_dec
+    return grad_dark, ge, gu, gw
 
 
 def solution(mesh):

time: 105 us -> 73.6 us (0.70)
  Pallas kernels: 80.8 us -> 65.1 us
  local copies, waits for them, and re-layouts: 23.3 us -> 7.61 us
    pallas_call x1, Pallas kernels: 80.8 us -> 65.1 us  [on_device(): pl.pallas_call(kernel, name='step', out_shape=(jax.ShapeDtypeStruct((512,...]
    reshape x8 -> x0, local copies, waits for them, and re-layouts: 9.14 us -> none  [the longest x1 2.08 us: on_device(): up_weight.reshape(64, 8, FCH, CH).transpose(0, 2, 1, 3).reshape(1024, 512)]
    transpose x6 -> x0, local copies, waits for them, and re-layouts: 3.24 us -> none  [the longest x1 2.13 us: on_device(): up_weight.reshape(64, 8, FCH, CH).transpose(0, 2, 1, 3).reshape(1024, 512)]
    rev x1 -> x0, local copies, waits for them, and re-layouts: 1.8 us -> none  [on_device(): wd = w_enc[::-1].reshape(9, 3 * CH, CH)]
    unnamed x32 -> x12, local copies, waits for them, and re-layouts: 8.29 us -> 7.61 us
where the time goes in v2:
time: 73.6 us; the launch traced here: 73.4 us
  Pallas kernels  65.1 us (88%)
  local copies, waits for them, and re-layouts  7.61 us (10%)
    pallas_call x1, Pallas kernels, on_device(): pl.pallas_call(kernel, name='step', out_shape=(jax.ShapeDtypeStruct((512,...  65.1 us
    unnamed x12, local copies, waits for them, and re-layouts  7.61 us

profile of v2, /device:TPU:1, one launch (start us, length us, event | category | flops | bytes accessed | tf_op | source)
XLA Modules:
  0.0 73.4 jit_solution(6391811046005503958)
XLA Ops:
  0.6 0.0 copy-start.1
  0.6 1.7 %copy.10.wdec = bf16[27,16,16]{2,1,0:T(8,128)(2,1)} copy(bf16[27,16,16]{0,2,1:T(8,128)(2,1)} %param.8) | data formatting | bytes 27648 | tf_op args[3]
  2.4 0.0 copy-done.1
  2.4 0.8 %copy.9 = bf16[27,16,16]{1,2,0:T(8,128)(2,1)} copy(bf16[27,16,16]{0,2,1:T(8,128)(2,1)S(1)} %copy-done.1) | data formatting | bytes 27648 | tf_op args[3]
  3.2 65.1 %step.1 = (f32[512,64]{1,0:T(8,128)}, f32[27,64,64]{2,1,0:T(8,128)}, f32[2,16,64]{2,1,0:T(8,128)}, f32[27,16,16]{2,1,0:T(8,128)}) custom-call(bf16[512,64]{1,0:T(8,128)(2,1)} %bitcast.15, bf16[27,64,64]{2,1,0:T(8,128)(2,1)} %wenc.1, bf16[16,64,512]{2,1,0:T(8,128)(2,1)} %bitcast.11, bf16[27,16,16]{2,1,0:T(8,128)(2,1)} %copy.10.wdec, ...), custom_call_target="tpu_custom_call" | custom-call | tf_op jit(solution)/shard_map/step/pallas_call | solution.py:540
  68.4 0.0 copy-start
  68.4 1.8 %copy.12 = f32[27,16,16]{0,2,1:T(8,128)} copy(f32[27,16,16]{2,1,0:T(8,128)} %get-tuple-element.15) | data formatting | bytes 55296
  70.2 1.7 %copy.16 = f32[64,32,1,16]{0,3,2,1:T(8,128)} copy(f32[64,32,1,16]{0,3,2,1:T(8,128)} %bitcast.13) | data formatting | bytes 262144
  71.9 0.0 copy-done
  71.9 0.0 copy-start.2
  71.9 0.9 %copy.17 = f32[27,64,64]{2,1,0:T(8,128)} copy(f32[27,64,64]{2,1,0:T(8,128)S(1)} %copy-done) | data formatting | bytes 884736
  72.8 0.0 copy-done.2
  72.8 0.6 copy.18
Async XLA Ops:
  0.6 1.7 %copy-start.1 = (bf16[27,16,16]{0,2,1:T(8,128)(2,1)S(1)}, bf16[27,16,16]{0,2,1:T(8,128)(2,1)}, u32[]{:S(2)}) copy-start(bf16[27,16,16]{0,2,1:T(8,128)(2,1)} %param.8) | copy-start | bytes 41476
  68.4 3.5 %copy-start = (f32[27,64,64]{2,1,0:T(8,128)S(1)}, f32[27,64,64]{2,1,0:T(8,128)}, u32[]{:S(2)}) copy-start(f32[27,64,64]{2,1,0:T(8,128)} %get-tuple-element.21) | copy-start | bytes 1327108
  71.9 0.9 %copy-start.2 = (f32[2,16,64]{2,1,0:T(8,128)S(1)}, f32[2,16,64]{2,1,0:T(8,128)}, u32[]{:S(2)}) copy-start(f32[2,16,64]{2,1,0:T(8,128)} %get-tuple-element.22) | copy-start | bytes 24580
